TPU v7x, 256 devices: a whole 4x4x8 slice. The times are simulated.
256 devices in a mesh: comp: 2 (over x_lo), panel: 4 (over x_hi, core), col: 32 (over z, y).
Axes of the slice: x: 4 (x_hi: 2, x_lo: 2; x = x_hi * 2 + x_lo), y: 4, z: 8, core: 2. Of those that a mesh axis runs over, the one named last changes fastest.
Arguments:
- joint_tracer_field: float32 [2, 2, 4, 2048, 1024], P('comp', None, None, 'col', 'panel'), may hold values from -5 to 5
- courant_mixing_rates: float32 [2, 3, 4, 2048, 1024], P('comp', None, None, 'col', 'panel'), may hold values from -0.24 to 0.24, as said below
- oceanic_indicator: int32 [2, 2048, 1024], P('comp', 'col', 'panel'), may hold values 0 or 1
- glacial_indicator: int32 [2048, 1024], P('col', 'panel'), may hold values 0 or 1
- prior_oceanic_warmth: float32 [2048, 1024], P('col', 'panel'), may hold values from -4 to 4
- prior_glacial_cover: float32 [2048, 1024], P('col', 'panel'), may hold values from 0 to 0.8
- partner_devices: int32 [16384, 2], P(('panel', 'col')), may hold values from 0 to 127, all different within a row; in each aligned block of 128 rows (0 to 127, 128 to 255, ...) at most 4 rows name the same one
- receiving_tile_index: int32 [16384, 2], P(('panel', 'col')), may hold values from 0 to 127
- bank_tile_entry: int32 [16384, 2], P(('panel', 'col')), may hold values from 0 to 31
- conservative_overlay_factors: float32 [32, 128, 128], replicated, may hold values from 0.002 to 0.014
Outputs:
- new_state: float32 [2, 2, 4, 2048, 1024], P('comp', None, None, 'col', 'panel')
- surface: float32 [2, 2, 2048, 1024], P('comp', None, 'col', 'panel')
Inputs may be any that keep to these rules, and one draw needn't show every extreme that they name: `partner_devices`: each row names two different ocean devices, device p * 32 + q lying at index p of panel and q of col. Among the 128 rows of one device no ocean device is named more than 4 times, and in the rows of some devices one is named exactly 4 times. courant_mixing_rates[c, 0] and courant_mixing_rates[c, 1] lie in [-0.24, 0.24]; courant_mixing_rates[c, 2] lies in [0.01, 0.24].
All inputs are finite; a program needn't handle non-finite values. No bound on the sum of `oceanic_indicator` or of `glacial_indicator` on one device may be relied on, other than what follows from the above.
Results may differ from a plain program's by a relative error of at most 0.00013.
Values sent between devices are 32-bit elements; how exact they have to be, the bound alone decides.
A program may use at most 64 MiB of HBM per device.

v0:
```python
import jax
import jax.numpy as jnp
from jax import lax
from jax.sharding import PartitionSpec as P

TILE = 128
NSUB = 4
HIGHEST = lax.Precision.HIGHEST


def passed_along(value, axis, steps):
    count = lax.axis_size(axis)
    initial, last = (max(0, -steps), min(count, count - steps))
    return lax.ppermute(value, axis, [(source, source + steps) for source in range(initial, last)])


def from_behind(array, axis, by):
    count = lax.axis_size(axis)
    return lax.ppermute(array, axis, [(i, (i + by) % count) for i in range(count)])


def wide_halo(array, width):
    west = from_behind(array[..., -width:], "panel", 1)
    east = from_behind(array[..., :width], "panel", -1)
    array = jnp.concatenate([west, array, east], axis=-1)
    south = passed_along(array[..., -width:, :], "col", 1)
    north = passed_along(array[..., :width, :], "col", -1)
    return jnp.concatenate([south, array, north], axis=-2)


def vertical_mix(tracer, mixing):
    level_flux = mixing[:-1] * (tracer[:, 1:] - tracer[:, :-1])
    zero_level = jnp.zeros_like(tracer[:, :1])
    from_above = jnp.concatenate([level_flux, zero_level], axis=1)
    from_below = jnp.concatenate([zero_level, level_flux], axis=1)
    relaxation = jnp.concatenate(
        [jnp.zeros_like(tracer[:, :-1]), mixing[-1:] * tracer[:, -1:]], axis=1
    )
    return tracer + from_above - from_below - relaxation


def advect_mix(tracer, east_vel, north_vel, mixing):
    centre = tracer[..., 1:-1, 1:-1]
    vel_east = east_vel[:, 1:-1, 1:-1]
    vel_west = east_vel[:, 1:-1, :-2]
    vel_north = north_vel[:, 1:-1, 1:-1]
    vel_south = north_vel[:, :-2, 1:-1]
    flux_east = (
        jnp.maximum(vel_east, 0.0) * centre + jnp.minimum(vel_east, 0.0) * tracer[..., 1:-1, 2:]
    )
    flux_west = (
        jnp.maximum(vel_west, 0.0) * tracer[..., 1:-1, :-2] + jnp.minimum(vel_west, 0.0) * centre
    )
    flux_north = (
        jnp.maximum(vel_north, 0.0) * centre + jnp.minimum(vel_north, 0.0) * tracer[..., 2:, 1:-1]
    )
    flux_south = (
        jnp.maximum(vel_south, 0.0) * tracer[..., :-2, 1:-1] + jnp.minimum(vel_south, 0.0) * centre
    )
    advanced = centre - (flux_east - flux_west) - (flux_north - flux_south)
    return vertical_mix(advanced, mixing[:, 1:-1, 1:-1])


def to_tiles(field_grid):
    fcount, grid_rows, grid_cols = field_grid.shape
    blocks = field_grid.reshape(fcount, grid_rows, grid_cols // TILE, TILE)
    return blocks.transpose(1, 2, 0, 3).reshape(-1, fcount, TILE)


def from_tiles(tile_form, grid_rows, grid_cols):
    fcount = tile_form.shape[1]
    blocks = tile_form.reshape(grid_rows, grid_cols // TILE, fcount, TILE)
    return blocks.transpose(2, 0, 1, 3).reshape(fcount, grid_rows, grid_cols)


def bucket_places(partner_devices, owners, capacity):
    owner_list = partner_devices.reshape(-1)
    owner_hit = (owner_list[:, None] == jnp.arange(owners, dtype=jnp.int32)[None, :]).astype(
        jnp.int32
    )
    owner_rank = jnp.cumsum(owner_hit, axis=0) - owner_hit
    position = jnp.sum(owner_rank * owner_hit, axis=1)
    return owner_list * capacity + position


def advect(start, coeffs, grid_rows):
    fields = start.shape[0] * start.shape[1]
    both = jnp.concatenate(
        [start.reshape((fields,) + start.shape[2:]), coeffs.reshape((-1,) + coeffs.shape[2:])]
    )
    wide = wide_halo(both, NSUB)
    levels = coeffs.shape[1]
    tracer = wide[:fields].reshape(start.shape[:2] + wide.shape[1:])
    coeff_ext = wide[fields:].reshape((3, levels) + wide.shape[1:])
    rows_total = grid_rows * lax.axis_size("col")
    row_global = (
        lax.axis_index("col") * grid_rows + jnp.arange(grid_rows + 2 * NSUB, dtype=jnp.int32) - NSUB
    )
    row_open = ((row_global >= 0) & (row_global < rows_total - 1)).astype(jnp.float32)
    east_ext = coeff_ext[0]
    north_ext = coeff_ext[1] * row_open[None, :, None]
    mix_ext = coeff_ext[2]
    for step_index in range(NSUB):
        s = step_index
        e = east_ext.shape[1] - s
        w = east_ext.shape[2] - s
        tracer = advect_mix(
            tracer, east_ext[:, s:e, s:w], north_ext[:, s:e, s:w], mix_ext[:, s:e, s:w]
        )
    return tracer


def on_device(
    joint_tracer_field,
    courant_mixing_rates,
    oceanic_indicator,
    glacial_indicator,
    prior_oceanic_warmth,
    prior_glacial_cover,
    partner_devices,
    receiving_tile_index,
    bank_tile_entry,
    conservative_overlay_factors,
):
    owners = lax.axis_size("panel") * lax.axis_size("col")
    tile_count = partner_devices.shape[0]
    capacity = max(2, 4 * tile_count // owners)
    slots = owners * capacity
    nbank = conservative_overlay_factors.shape[0]
    on_atmos = lax.axis_index("comp") == 0
    device_tracer_share = joint_tracer_field[0]
    coeffs = courant_mixing_rates[0]
    grid_rows = coeffs.shape[2]
    grid_cols = coeffs.shape[3]
    sea_here = oceanic_indicator[0].astype(jnp.float32)
    wind_east = coeffs[0, 0]
    wind_north = coeffs[1, 0]
    airflow_speed = jnp.sqrt(wind_east * wind_east + wind_north * wind_north + 0.01)
    unfrozen_share = sea_here * (1.0 - prior_glacial_cover)
    thermal_exchange_rate = (
        2.0 * airflow_speed * (prior_oceanic_warmth - device_tracer_share[0, 0]) * unfrozen_share
    )
    evaporation_rate = (
        2.0
        * airflow_speed
        * (jnp.exp(0.1 * prior_oceanic_warmth) - device_tracer_share[1, 0])
        * unfrozen_share
    )
    heated = device_tracer_share.at[0, 0].add(thermal_exchange_rate).at[1, 0].add(evaporation_rate)
    start = jnp.where(on_atmos, heated, device_tracer_share)
    surface_flux = jnp.stack([thermal_exchange_rate, evaporation_rate])
    flux_rows = passed_along(to_tiles(surface_flux), "comp", 1).reshape(tile_count * 2, TILE)
    pairs = tile_count * 2
    bucket_place = bucket_places(partner_devices, owners, capacity)
    place_match = bucket_place[None, :] == jnp.arange(slots, dtype=jnp.int32)[:, None]
    slot_used = jnp.any(place_match, axis=1)
    slot_pair = jnp.sum(
        jnp.where(place_match, jnp.arange(pairs, dtype=jnp.int32)[None, :], 0), axis=1
    )
    slot_tile = slot_pair // 2
    slot_bank = jnp.sum(jnp.where(place_match, bank_tile_entry.reshape(-1)[None, :], 0), axis=1)
    by_bank = jnp.einsum(
        "bji,ri->brj", conservative_overlay_factors, flux_rows, precision=lax.Precision.HIGH
    ).reshape(nbank * pairs, TILE)
    f_ids = jnp.arange(2, dtype=jnp.int32)[None, :]
    slot_rows = (slot_bank * pairs + slot_tile * 2)[:, None] + f_ids
    picked = by_bank[slot_rows.reshape(-1)].reshape(slots, 2, TILE)
    buffer = jnp.where(slot_used[:, None, None], picked, 0.0).reshape(owners, capacity * 2, TILE)
    received = lax.all_to_all(buffer, ("panel", "col"), 0, 0, tiled=True).reshape(slots * 2, TILE)
    me = lax.axis_index("panel") * lax.axis_size("col") + lax.axis_index("col")
    own_routes = jnp.concatenate([partner_devices.T, receiving_tile_index.T], axis=0)
    owner_ids = jnp.arange(owners, dtype=jnp.int32)[:, None, None]
    routes = lax.psum(
        jnp.where(owner_ids == me, own_routes[None].astype(jnp.float32), 0.0), ("panel", "col")
    ).astype(jnp.int32)
    mine = [(routes[:, k] == me).astype(jnp.int32) for k in range(2)]
    per_tile = mine[0] + mine[1]
    before = jnp.cumsum(per_tile, axis=1) - per_tile
    rank = [before, before + mine[0]]
    recv_slots = jnp.stack(
        [
            sum((jnp.sum(mine[k] * (rank[k] == c) * routes[:, 2 + k], axis=1) for k in range(2)))
            for c in range(capacity)
        ],
        axis=1,
    ).reshape(-1)
    row_ids = lax.broadcasted_iota(jnp.int32, (pairs, slots * 2), 0)
    col_ids = lax.broadcasted_iota(jnp.int32, (pairs, slots * 2), 1)
    recv_rep = jnp.broadcast_to(recv_slots[:, None], (slots, 2)).reshape(-1)
    slot_hit2 = ((recv_rep[None, :] == row_ids // 2) & (col_ids % 2 == row_ids % 2)).astype(
        jnp.float32
    )
    summed = jnp.dot(slot_hit2, received, precision=HIGHEST)
    forcing = from_tiles(summed.reshape(tile_count, 2, TILE), grid_rows, grid_cols)
    tracer = advect(start, coeffs, grid_rows)
    forced = (
        tracer.at[0, 0]
        .add(-(0.5 * sea_here * forcing[0]))
        .at[1, 0]
        .add(0.5 * sea_here * forcing[1])
    )
    new_here = jnp.where(on_atmos, tracer, forced)
    sea_temp = new_here[0, 0]
    ice_cover = (
        glacial_indicator.astype(jnp.float32) * sea_here * jnp.clip(0.5 - sea_temp, 0.0, 1.0)
    )
    ocean_surface = jnp.stack([sea_temp, ice_cover])
    ocean_tiles = to_tiles(ocean_surface).reshape(pairs, TILE)
    reply = jnp.dot(slot_hit2.T, ocean_tiles, precision=HIGHEST).reshape(owners, capacity * 2, TILE)
    returned = lax.all_to_all(reply, ("panel", "col"), 0, 0, tiled=True).reshape(slots * 2, TILE)
    place_rep = jnp.broadcast_to(bucket_place[:, None], (pairs, 2)).reshape(-1)
    p_rows = lax.broadcasted_iota(jnp.int32, (pairs * 2, slots * 2), 0)
    p_cols = lax.broadcasted_iota(jnp.int32, (pairs * 2, slots * 2), 1)
    place_hit2 = ((place_rep[:, None] == p_cols // 2) & (p_cols % 2 == p_rows % 2)).astype(
        jnp.float32
    )
    values = jnp.dot(place_hit2, returned, precision=HIGHEST)
    by_bank_back = jnp.einsum(
        "rj,bji->bri", values, conservative_overlay_factors, precision=lax.Precision.HIGH
    ).reshape(nbank * pairs * 2, TILE)
    tile_ids = jnp.arange(tile_count, dtype=jnp.int32)[:, None]
    pair_rows = (bank_tile_entry * tile_count + tile_ids) * 4 + jnp.arange(2, dtype=jnp.int32)[
        None, :
    ] * 2
    back_rows = pair_rows[:, :, None] + f_ids[:, None, :]
    numerator = jnp.sum(by_bank_back[back_rows.reshape(-1)].reshape(tile_count, 2, 2, TILE), axis=1)
    column_sums = jnp.sum(conservative_overlay_factors, axis=1)
    bank_ids = jnp.arange(nbank, dtype=jnp.int32)[None, :]
    bank_count = (bank_tile_entry[:, :1] == bank_ids).astype(jnp.float32) + (
        bank_tile_entry[:, 1:] == bank_ids
    ).astype(jnp.float32)
    denominator = jnp.dot(bank_count, column_sums, precision=HIGHEST)
    remap_back = numerator / denominator[:, None, :]
    remapped = passed_along(from_tiles(remap_back, grid_rows, grid_cols), "comp", -1)
    surface_here = jnp.where(on_atmos, remapped, ocean_surface)
    return (new_here[None], surface_here[None])


def solution(mesh):
    return jax.shard_map(
        on_device,
        mesh=mesh,
        in_specs=(
            P("comp", None, None, "col", "panel"),
            P("comp", None, None, "col", "panel"),
            P("comp", "col", "panel"),
            P("col", "panel"),
            P("col", "panel"),
            P("col", "panel"),
            P(("panel", "col"), None),
            P(("panel", "col"), None),
            P(("panel", "col"), None),
            P(),
        ),
        out_specs=(P("comp", None, None, "col", "panel"), P("comp", None, "col", "panel")),
        check_vma=False,
    )
```

profile of v0, /device:TPU:1, one launch (start us, length us, event | category | flops | bytes accessed | tf_op | source)
XLA Modules:
  0.0 1241.6 jit_solution(11290199410697722666)
XLA Ops:
  7.2 2.1 copy.125
  10.3 1.5 bitcast_dynamic-update-slice_fusion
  11.8 1.7 fusion.81
  13.5 1.3 broadcast_select_fusion.1
  14.8 1.3 fusion.48
  16.1 2.0 copy.93
  18.1 3.2 collective-permute-start.1
  21.3 2.0 copy.92
  26.5 3.5 collective-permute-start.4
  41.1 1.2 reduce-window.9
  44.8 1.1 add.421
  48.8 1.9 copy.95
  50.7 1.9 copy.94
  52.6 1.3 pad_maximum_fusion.8
  54.0 1.3 collective-permute-start.3
  55.3 4.2 collective-permute-start.2
  59.7 1.5 collective-permute-done.3
  61.1 1.3 collective-permute-done.2
  74.5 5.1 fusion.135
  79.6 5.0 gather_fusion
  85.6 18.1 %all-to-all-start = ((f32[128,8,128]{2,1,0:T(8,128)}), f32[128,8,128]{2,1,0:T(8,128)}, u32[]{:S(2)}, u32[]{:S(2)}) async-start(f32[128,8,128]{2,1,0:T(8,128)} %bitcast_select_fusion), calls=%async_computation | async-start | bytes 1048576 | tf_op jit(solution)/shard_map/all_to_all | solution.py:169
  103.7 1047.6 %all-reduce.14.cloned.1.call-done = f32[128,4,128]{0,2,1:T(8,128)} async-done(((f32[128,4,128]{0,2,1:T(8,128)}), f32[128,4,128]{0,2,1:T(8,128)}) %all-reduce.14.cloned.1.call-update) | async-done | bytes 262160 | tf_op jit(solution)/shard_map/psum | solution.py:173
  1153.3 1.5 fusion.15
  1154.8 1.9 convolution_bitcast_fusion
  1158.1 1.5 fusion.17
  1159.6 36.4 %all-to-all-start.1 = ((f32[128,8,128]{2,1,0:T(8,128)}), f32[128,8,128]{2,1,0:T(8,128)S(1)}, u32[]{:S(2)}, u32[]{:S(2)}) async-start(f32[128,8,128]{2,1,0:T(8,128)} %fusion.17), calls=%async_computation.1 | async-start | bytes 1048576 | tf_op jit(solution)/shard_map/all_to_all | solution.py:210
  1197.5 18.6 %all-to-all-done.1 = f32[128,8,128]{2,1,0:T(8,128)S(1)} async-done(((f32[128,8,128]{2,1,0:T(8,128)}), f32[128,8,128]{2,1,0:T(8,128)S(1)}, u32[]{:S(2)}, u32[]{:S(2)}) %all-to-all-start.1) | async-done | bytes 524320 | tf_op jit(solution)/shard_map/all_to_all | solution.py:210
  1216.1 1.2 fusion.3
  1217.3 5.6 fusion.136
  1222.9 4.4 gather_fusion.1
  1227.8 1.3 collective-permute-start.5
  1229.1 5.0 collective-permute-done.5
  (194 shorter events, 39.2 us)
Async XLA Ops:
  7.2 67.3 %copy-start = (f32[32,128,128]{2,1,0:T(8,128)S(1)}, f32[32,128,128]{2,1,0:T(8,128)}, u32[]{:S(2)}) copy-start(f32[32,128,128]{2,1,0:T(8,128)} %param.27) | copy-start | bytes 6291460
  7.2 7.6 copy-start.1
  7.2 1144.2 %all-reduce.14.cloned.1.call-start = ((), (), s32[]{:S(2)}) async-start(), calls=%async_computation.2 | async-start | bytes 524288 | tf_op jit(solution)/shard_map/psum | solution.py:173
  14.8 15.3 %copy-start.22 = (s32[128,2]{0,1:T(2,128)S(1)}, s32[128,2]{0,1:T(2,128)}, u32[]{:S(2)}) copy-start(s32[128,2]{0,1:T(2,128)} %param.24) | copy-start | bytes 3076
  14.8 15.2 %copy-start.28 = (s32[128,2]{0,1:T(2,128)S(1)}, s32[128,2]{0,1:T(2,128)}, u32[]{:S(2)}) copy-start(s32[128,2]{0,1:T(2,128)} %param.25) | copy-start | bytes 3076
  18.1 25.2 %copy-start.15 = (s32[128,2]{0,1:T(2,128)S(1)}, s32[128,2]{0,1:T(2,128)}, u32[]{:S(2)}) copy-start(s32[128,2]{0,1:T(2,128)} %param.26) | copy-start | bytes 3076
  18.1 30.7 %collective-permute-start.1 = (f32[20,64,4]{1,2,0:T(4,128)}, f32[20,64,4]{1,2,0:T(4,128)}, u32[]{:S(2)}, u32[]{:S(2)}) collective-permute-start(f32[20,64,4]{1,2,0:T(4,128)} %copy.93), channel_id=1, source_target_pairs={{0,96},{32,0},{64,32},{96,64},{1,97},{33,1},{65,33},{97,65},{2,98}... | collective-permute-start | bytes 61448 | tf_op jit(solution)/shard_map/ppermute | solution.py:19
  23.2 27.5 %collective-permute-start = (f32[20,64,4]{1,2,0:T(4,128)}, f32[20,64,4]{1,2,0:T(4,128)}, u32[]{:S(2)}, u32[]{:S(2)}) collective-permute-start(f32[20,64,4]{1,2,0:T(4,128)} %copy.92), channel_id=1, source_target_pairs={{0,32},{32,64},{64,96},{96,0},{1,33},{33,65},{65,97},{97,1},{2,34}... | collective-permute-start | bytes 61448 | tf_op jit(solution)/shard_map/ppermute | solution.py:19
  26.5 47.9 %collective-permute-start.4 = (f32[128,2,128]{2,1,0:T(2,128)}, f32[128,2,128]{2,1,0:T(2,128)}, u32[]{:S(2)}, u32[]{:S(2)}) collective-permute-start(f32[128,2,128]{2,1,0:T(2,128)} %bitcast.33), channel_id=1, source_target_pairs={{0,128},{1,129},{2,130},{3,131},{4,132},{5,133},{6,134},{7,135},{8... | collective-permute-start | bytes 393224 | tf_op jit(solution)/shard_map/ppermute | solution.py:14
  52.6 6.8 copy-start.2
  52.6 9.8 copy-start.3
  54.0 7.1 collective-permute-start.3
  55.3 7.1 collective-permute-start.2
  74.5 5.1 copy-start.4
  84.6 1068.7 %copy-start.18 = (s32[256]{0:T(256)S(1)}, s32[256]{0:T(256)}, u32[]{:S(2)}) copy-start(s32[256]{0:T(256)} %get-tuple-element.138) | copy-start | bytes 3076
  84.6 1068.7 %copy-start.19 = (s32[256]{0:T(256)S(1)}, s32[256]{0:T(256)}, u32[]{:S(2)}) copy-start(s32[256]{0:T(256)} %get-tuple-element.139) | copy-start | bytes 3076
  84.6 1068.7 %copy-start.20 = (s32[256]{0:T(256)S(1)}, s32[256]{0:T(256)}, u32[]{:S(2)}) copy-start(s32[256]{0:T(256)} %get-tuple-element.140) | copy-start | bytes 3076
  84.6 1068.7 %copy-start.21 = (s32[256]{0:T(256)S(1)}, s32[256]{0:T(256)}, u32[]{:S(2)}) copy-start(s32[256]{0:T(256)} %get-tuple-element.141) | copy-start | bytes 3076
  84.6 1070.2 %copy-start.23 = (s32[1024]{0:T(1024)S(1)}, s32[1024]{0:T(1024)}, u32[]{:S(2)}) copy-start(s32[1024]{0:T(1024)} %get-tuple-element.128) | copy-start | bytes 12292
  84.6 1070.2 %copy-start.25 = (s32[1024]{0:T(1024)S(1)}, s32[1024]{0:T(1024)}, u32[]{:S(2)}) copy-start(s32[1024]{0:T(1024)} %get-tuple-element.129) | copy-start | bytes 12292
  84.6 1070.2 %copy-start.27 = (s32[64,2,2]{0,2,1:T(2,128)S(1)}, s32[64,2,2]{0,2,1:T(2,128)}, u32[]{:S(2)}) copy-start(s32[64,2,2]{0,2,1:T(2,128)} %get-tuple-element.134) | copy-start | bytes 3076
  85.6 1069.2 %all-to-all-start = ((f32[128,8,128]{2,1,0:T(8,128)}), f32[128,8,128]{2,1,0:T(8,128)}, u32[]{:S(2)}, u32[]{:S(2)}) async-start(f32[128,8,128]{2,1,0:T(8,128)} %bitcast_select_fusion), calls=%async_computation | async-start | bytes 1048576 | tf_op jit(solution)/shard_map/all_to_all | solution.py:169
  1152.6 4.3 copy-start.6
  1152.6 4.3 copy-start.9
  1153.0 4.0 copy-start.5
  1156.9 39.1 %copy-start.17 = (s32[256]{0:T(256)S(1)}, s32[256]{0:T(256)}, u32[]{:S(2)}) copy-start(s32[256]{0:T(256)} %copy-done.16) | copy-start | bytes 3076
  1157.0 39.2 %copy-start.12 = (s32[128,2,2]{2,1,0:T(2,128)S(1)}, s32[128,2,2]{2,1,0:T(2,128)}, u32[]{:S(2)}) copy-start(s32[128,2,2]{2,1,0:T(2,128)} %iota_add_fusion.1) | copy-start | bytes 6148
  1158.1 58.0 %copy-start.24 = (s32[1024]{0:T(1024)S(1)}, s32[1024]{0:T(1024)}, u32[]{:S(2)}) copy-start(s32[1024]{0:T(1024)} %get-tuple-element.128) | copy-start | bytes 12292
  1158.1 58.0 %copy-start.26 = (s32[1024]{0:T(1024)S(1)}, s32[1024]{0:T(1024)}, u32[]{:S(2)}) copy-start(s32[1024]{0:T(1024)} %get-tuple-element.129) | copy-start | bytes 12292
  1158.1 58.0 %copy-start.29 = (pred[1024]{0:T(1024)(128)(4,1)S(1)}, pred[1024]{0:T(1024)(128)(4,1)}, u32[]{:S(2)}) copy-start(pred[1024]{0:T(1024)(128)(4,1)} %fusion.121) | copy-start | bytes 3076
  1159.6 56.4 %all-to-all-start.1 = ((f32[128,8,128]{2,1,0:T(8,128)}), f32[128,8,128]{2,1,0:T(8,128)S(1)}, u32[]{:S(2)}, u32[]{:S(2)}) async-start(f32[128,8,128]{2,1,0:T(8,128)} %fusion.17), calls=%async_computation.1 | async-start | bytes 1048576 | tf_op jit(solution)/shard_map/all_to_all | solution.py:210
  1227.8 6.3 collective-permute-start.5
  (7 other events, 10.4 us)
Sparse Core Ops, SparseCore 0:
  31.1 1120.2 all-reduce.13
where the time goes:
time: 1240 us
  waiting for transfers between devices  1070 us (86%)
  starting transfers between devices  69 us (6%)
  other arithmetic  38.4 us (3%)
  local copies, waits for them, and re-layouts  29.6 us (2%)
  matrix products  15.6 us (1%)
  between operations  15 us (1%)
    psum x1, waiting for transfers between devices, on_device(): lax.psum(jnp.where(owner_ids == me, own_routes[None].astype(jnp.float32),...  1050 us
    all_to_all x1, starting transfers between devices, on_device(): lax.all_to_all(reply, ('panel', 'col'), 0, 0, tiled=True)  36.4 us
  transfers between devices with their start and end apart: 9, of which 5 were waited for; matrix products, arithmetic and copies ran while one was open for 4% of the time, Pallas kernels for 0%

commit v1 on v0

--- a/solution.py
+++ b/solution.py
@@ -170,8 +170,11 @@
     me = lax.axis_index("panel") * lax.axis_size("col") + lax.axis_index("col")
     own_routes = jnp.concatenate([partner_devices.T, receiving_tile_index.T], axis=0)
     owner_ids = jnp.arange(owners, dtype=jnp.int32)[:, None, None]
-    routes = lax.psum(
-        jnp.where(owner_ids == me, own_routes[None].astype(jnp.float32), 0.0), ("panel", "col")
+    routes = jnp.sum(
+        lax.all_gather(
+            jnp.where(owner_ids == me, own_routes[None].astype(jnp.float32), 0.0), ("panel", "col")
+        ),
+        axis=0,
     ).astype(jnp.int32)
     mine = [(routes[:, k] == me).astype(jnp.int32) for k in range(2)]
     per_tile = mine[0] + mine[1]

time: 1240 us -> 312 us (0.25)
  waiting for transfers between devices: 1070 us -> 158 us
  starting transfers between devices: 69 us -> 41.6 us
    psum x1 -> x0, waiting for transfers between devices: 1050 us -> none  [on_device(): lax.psum(jnp.where(owner_ids == me, own_routes[None].astype(jnp.float32),...]
    all_gather x0 -> x1, waiting for transfers between devices: none -> 130 us  [on_device(): lax.all_gather(jnp.where(owner_ids == me, own_routes[None].astype(jnp.flo...]
    all_to_all x1, starting transfers between devices: 36.4 us -> 8.42 us  [on_device(): lax.all_to_all(reply, ('panel', 'col'), 0, 0, tiled=True)]
  transfers between devices with their start and end apart: 9 -> 9, of which waited for: 5 -> 5; matrix products, arithmetic and copies ran while one was open for 4% -> 24% of each run, Pallas kernels for 0% -> 0%
where the time goes in v1:
time: 312 us; the launch traced here: 311 us
  waiting for transfers between devices  158 us (51%)
  other arithmetic  50.8 us (16%)
  starting transfers between devices  41.6 us (13%)
  local copies, waits for them, and re-layouts  30 us (10%)
  matrix products  15.6 us (5%)
  between operations  15.2 us (5%)
    all_gather x1, waiting for transfers between devices, on_device(): lax.all_gather(jnp.where(owner_ids == me, own_routes[None].astype(jnp.flo...  130 us
    all_to_all x1, starting transfers between devices, on_device(): lax.all_to_all(buffer, ('panel', 'col'), 0, 0, tiled=True)  19.3 us
    all_to_all x1, waiting for transfers between devices, on_device(): lax.all_to_all(reply, ('panel', 'col'), 0, 0, tiled=True)  18.6 us
    reduce_sum x1, other arithmetic, on_device(): jnp.sum(lax.all_gather(jnp.where(owner_ids == me, own_routes[None].astype...  12 us
    ppermute x4, starting transfers between devices, passed_along(): lax.ppermute(value, axis, [(source, source + steps) for source in range(i...  10.6 us
    ppermute x4, waiting for transfers between devices, passed_along(): lax.ppermute(value, axis, [(source, source + steps) for source in range(i...  8.96 us
    all_to_all x1, starting transfers between devices, on_device(): lax.all_to_all(reply, ('panel', 'col'), 0, 0, tiled=True)  8.42 us
  transfers between devices with their start and end apart: 9, of which 5 were waited for; matrix products, arithmetic and copies ran while one was open for 24% of the time, Pallas kernels for 0%

profile of v1, /device:TPU:1, one launch (start us, length us, event | category | flops | bytes accessed | tf_op | source)
XLA Modules:
  0.0 311.0 jit_solution(2105529935306060497)
XLA Ops:
  9.0 1.0 copy.153
  10.0 1.0 fusion.84
  15.3 4.6 %collective-permute-start.4 = (f32[128,2,128]{2,1,0:T(2,128)}, f32[128,2,128]{2,1,0:T(2,128)}, u32[]{:S(2)}, u32[]{:S(2)}) collective-permute-start(f32[128,2,128]{2,1,0:T(2,128)} %bitcast.33), channel_id=1, source_target_pairs={{0,128},{1,129},{2,130},{3,131},{4,132},{5,133},{6,134},{7,135},{8... | collective-permute-start | bytes 393224 | tf_op jit(solution)/shard_map/ppermute | solution.py:14
  19.9 1.3 broadcast_select_fusion.1
  21.2 1.3 fusion.48
  22.5 2.0 copy.119
  24.5 3.3 %collective-permute-start = (f32[20,64,4]{1,2,0:T(4,128)}, f32[20,64,4]{1,2,0:T(4,128)}, u32[]{:S(2)}, u32[]{:S(2)}) collective-permute-start(f32[20,64,4]{1,2,0:T(4,128)} %copy.119), channel_id=1, source_target_pairs={{0,32},{32,64},{64,96},{96,0},{1,33},{33,65},{65,97},{97,1},{2,34}... | collective-permute-start | bytes 61448 | tf_op jit(solution)/shard_map/ppermute | solution.py:19
  27.8 2.0 copy.120
  30.9 1.0 fusion.71
  32.8 1.5 broadcast_in_dim.81
  36.3 1.1 add.419
  47.1 1.9 copy.121
  49.0 1.9 copy.122
  50.9 1.3 pad_maximum_fusion.8
  52.2 3.2 %collective-permute-start.2 = (f32[20,4,264]{2,1,0:T(4,128)S(1)}, f32[20,4,264]{2,1,0:T(4,128)S(1)}, u32[]{:S(2)}, u32[]{:S(2)}) collective-permute-start(f32[20,4,264]{2,1,0:T(4,128)S(1)} %get-tuple-element.71), channel_id=1, source_target_pairs={{0,1},{1,2},{2,3},{3,4},{4,5},{5,6},{6,7},{7,8},{8,9},{9,10},{10,1... | collective-permute-start | bytes 253448 | tf_op jit(solution)/shard_map/ppermute | solution.py:14
  55.4 1.5 collective-permute-start.3
  57.3 3.8 %collective-permute-done.3 = f32[20,4,264]{2,1,0:T(4,128)S(1)} collective-permute-done((f32[20,4,264]{2,1,0:T(4,128)S(1)}, f32[20,4,264]{2,1,0:T(4,128)S(1)}, u32[]{:S(2)}, u32[]{:S(2)}) %collective-permute-start.3) | collective-permute-done | bytes 84512 | tf_op jit(solution)/shard_map/ppermute | solution.py:14
  74.2 5.0 %fusion.135 = f32[256,32,128]{2,0,1:T(8,128)} fusion(f32[256,128,1]{1,0,2:T(8,128)} %bitcast.35, f32[32,128,128]{2,1,0:T(8,128)S(1)} %copy-done), kind=kOutput, calls=%fused_computation.307 | convolution fusion | flops 805306368 | bytes 6422528 | tf_op jit(solution)/shard_map/bji,ri->brj/dot_general | solution.py:162
  79.2 5.0 %gather_fusion = f32[1024,128]{1,0:T(8,128)S(1)} fusion(f32[8192,128]{1,0:T(8,128)} %bitcast.285, s32[1024]{0:T(1024)S(1)} %broadcast_clamp_fusion), kind=kCustom, calls=%fused_computation | custom fusion | bytes 1052672 | tf_op jit(solution)/shard_map/gather | solution.py:167
  85.2 19.3 %all-to-all-start = ((f32[128,8,128]{2,1,0:T(8,128)}), f32[128,8,128]{2,1,0:T(8,128)}, u32[]{:S(2)}, u32[]{:S(2)}) async-start(f32[128,8,128]{2,1,0:T(8,128)} %bitcast_select_fusion), calls=%async_computation | async-start | bytes 1048576 | tf_op jit(solution)/shard_map/all_to_all | solution.py:169
  104.6 2.4 pad_subtract_fusion.3
  107.0 130.3 %all-gather.2.cloned.1.call-done = f32[128,128,4,128]{3,1,2,0:T(8,128)} async-done(((f32[1,128,4,128]{3,1,2,0:T(8,128)}), f32[128,128,4,128]{3,1,2,0:T(8,128)}) %all-gather.2.cloned.1.call-update) | async-done | bytes 33554448 | tf_op jit(solution)/shard_map/all_gather | solution.py:174
  237.3 12.0 %reduce_sum.128 = f32[128,4,128]{2,0,1:T(8,128)S(1)} reduce(f32[128,128,4,128]{3,1,2,0:T(8,128)} %all-gather.2.cloned.1.call-done, f32[]{:T(128)} %constant.263.clone.1), dimensions={0}, to_apply=%region_0.0 | reduce | flops 8323072 | bytes 33816580 | tf_op jit(solution)/shard_map/reduce_sum | solution.py:173
  250.4 1.9 convolution_bitcast_fusion
  255.4 1.5 fusion.17
  257.0 8.4 %all-to-all-start.1 = ((f32[128,8,128]{2,1,0:T(8,128)}), f32[128,8,128]{2,1,0:T(8,128)S(1)}, u32[]{:S(2)}, u32[]{:S(2)}) async-start(f32[128,8,128]{2,1,0:T(8,128)} %fusion.17), calls=%async_computation.1 | async-start | bytes 1048576 | tf_op jit(solution)/shard_map/all_to_all | solution.py:213
  266.9 18.6 %all-to-all-done.1 = f32[128,8,128]{2,1,0:T(8,128)S(1)} async-done(((f32[128,8,128]{2,1,0:T(8,128)}), f32[128,8,128]{2,1,0:T(8,128)S(1)}, u32[]{:S(2)}, u32[]{:S(2)}) %all-to-all-start.1) | async-done | bytes 524320 | tf_op jit(solution)/shard_map/all_to_all | solution.py:213
  285.5 1.2 fusion.3
  286.7 5.6 %fusion.136 = f32[512,32,128]{2,0,1:T(8,128)} fusion(f32[512,128,1]{1,0,2:T(8,128)S(1)} %fusion.3, f32[32,128,128]{2,1,0:T(8,128)S(1)} %copy-done), kind=kOutput, calls=%fused_computation.308 | convolution fusion | flops 1610612736 | bytes 10747904 | tf_op jit(solution)/shard_map/rj,bji->bri/dot_general | solution.py:221
  292.3 4.4 %gather_fusion.1 = f32[512,128]{1,0:T(8,128)S(1)} fusion(f32[16384,128]{1,0:T(8,128)} %bitcast.286, s32[1024]{0:T(1024)S(1)} %pad_clamp_fusion), kind=kCustom, calls=%fused_computation.1 | custom fusion | bytes 526336 | tf_op jit(solution)/shard_map/gather | solution.py:229
  297.2 1.3 collective-permute-start.5
  298.5 5.0 %collective-permute-done.5 = f32[2,64,256]{2,1,0:T(8,128)S(1)} collective-permute-done((f32[2,64,256]{2,1,0:T(8,128)S(1)}, f32[2,64,256]{2,1,0:T(8,128)S(1)}, u32[]{:S(2)}, u32[]{:S(2)}) %collective-permute-start.5) | collective-permute-done | bytes 131104 | tf_op jit(solution)/shard_map/ppermute | solution.py:14
  (208 shorter events, 40.1 us)
Async XLA Ops:
  7.2 67.0 %copy-start = (f32[32,128,128]{2,1,0:T(8,128)S(1)}, f32[32,128,128]{2,1,0:T(8,128)}, u32[]{:S(2)}) copy-start(f32[32,128,128]{2,1,0:T(8,128)} %param.27) | copy-start | bytes 6291460
  7.2 5.4 %copy-start.1 = (f32[1,3,4,64,256]{4,3,2,1,0:T(8,128)S(1)}, f32[1,3,4,64,256]{4,3,2,1,0:T(8,128)}, u32[]{:S(2)}) copy-start(f32[1,3,4,64,256]{4,3,2,1,0:T(8,128)} %param.19) | copy-start | bytes 2359300
  7.2 5.4 %copy-start.16 = (s32[1,64,256]{2,1,0:T(8,128)S(1)}, s32[1,64,256]{2,1,0:T(8,128)}, u32[]{:S(2)}) copy-start(s32[1,64,256]{2,1,0:T(8,128)} %param.20) | copy-start | bytes 196612
  7.2 230.1 %all-gather.2.cloned.1.call-start = ((), (), s32[]{:S(2)}) async-start(), calls=%async_computation.2 | async-start | bytes 33816576 | tf_op jit(solution)/shard_map/all_gather | solution.py:174
  13.6 6.4 %copy-start.7 = (f32[2,4,64,256]{3,2,1,0:T(8,128)}, f32[2,4,64,256]{3,2,1,0:T(8,128)S(1)}, u32[]{:S(2)}) copy-start(f32[2,4,64,256]{3,2,1,0:T(8,128)S(1)} %get-tuple-element.69) | copy-start | bytes 1572868
  15.3 58.8 %collective-permute-start.4 = (f32[128,2,128]{2,1,0:T(2,128)}, f32[128,2,128]{2,1,0:T(2,128)}, u32[]{:S(2)}, u32[]{:S(2)}) collective-permute-start(f32[128,2,128]{2,1,0:T(2,128)} %bitcast.33), channel_id=1, source_target_pairs={{0,128},{1,129},{2,130},{3,131},{4,132},{5,133},{6,134},{7,135},{8... | collective-permute-start | bytes 393224 | tf_op jit(solution)/shard_map/ppermute | solution.py:14
  21.2 8.5 %copy-start.29 = (s32[128,2]{0,1:T(2,128)S(1)}, s32[128,2]{0,1:T(2,128)}, u32[]{:S(2)}) copy-start(s32[128,2]{0,1:T(2,128)} %param.24) | copy-start | bytes 3076
  21.2 10.8 %copy-start.22 = (s32[128,2]{0,1:T(2,128)S(1)}, s32[128,2]{0,1:T(2,128)}, u32[]{:S(2)}) copy-start(s32[128,2]{0,1:T(2,128)} %param.26) | copy-start | bytes 3076
  24.5 22.6 %collective-permute-start = (f32[20,64,4]{1,2,0:T(4,128)}, f32[20,64,4]{1,2,0:T(4,128)}, u32[]{:S(2)}, u32[]{:S(2)}) collective-permute-start(f32[20,64,4]{1,2,0:T(4,128)} %copy.119), channel_id=1, source_target_pairs={{0,32},{32,64},{64,96},{96,0},{1,33},{33,65},{65,97},{97,1},{2,34}... | collective-permute-start | bytes 61448 | tf_op jit(solution)/shard_map/ppermute | solution.py:19
  29.7 19.2 %collective-permute-start.1 = (f32[20,64,4]{1,2,0:T(4,128)}, f32[20,64,4]{1,2,0:T(4,128)}, u32[]{:S(2)}, u32[]{:S(2)}) collective-permute-start(f32[20,64,4]{1,2,0:T(4,128)} %copy.120), channel_id=1, source_target_pairs={{0,96},{32,0},{64,32},{96,64},{1,97},{33,1},{65,33},{97,65},{2,98}... | collective-permute-start | bytes 61448 | tf_op jit(solution)/shard_map/ppermute | solution.py:19
  34.5 9.1 %copy-start.23 = (s32[256]{0:T(256)}, s32[256]{0:T(256)S(1)}, u32[]{:S(2)}) copy-start(s32[256]{0:T(256)S(1)} %multiply_add_fusion.2) | copy-start | bytes 3076
  50.9 6.1 %copy-start.2 = (f32[20,64,4]{2,1,0:T(8,128)S(1)}, f32[20,64,4]{2,1,0:T(8,128)}, u32[]{:S(2)}) copy-start(f32[20,64,4]{2,1,0:T(8,128)} %copy.121) | copy-start | bytes 61444
  50.9 10.2 %copy-start.3 = (f32[20,64,4]{2,1,0:T(8,128)S(1)}, f32[20,64,4]{2,1,0:T(8,128)}, u32[]{:S(2)}) copy-start(f32[20,64,4]{2,1,0:T(8,128)} %copy.122) | copy-start | bytes 61444
  52.2 5.1 %collective-permute-start.2 = (f32[20,4,264]{2,1,0:T(4,128)S(1)}, f32[20,4,264]{2,1,0:T(4,128)S(1)}, u32[]{:S(2)}, u32[]{:S(2)}) collective-permute-start(f32[20,4,264]{2,1,0:T(4,128)S(1)} %get-tuple-element.71), channel_id=1, source_target_pairs={{0,1},{1,2},{2,3},{3,4},{4,5},{5,6},{6,7},{7,8},{8,9},{9,10},{10,1... | collective-permute-start | bytes 253448 | tf_op jit(solution)/shard_map/ppermute | solution.py:14
  55.4 5.6 %collective-permute-start.3 = (f32[20,4,264]{2,1,0:T(4,128)S(1)}, f32[20,4,264]{2,1,0:T(4,128)S(1)}, u32[]{:S(2)}, u32[]{:S(2)}) collective-permute-start(f32[20,4,264]{2,1,0:T(4,128)S(1)} %get-tuple-element.72), channel_id=1, source_target_pairs={{1,0},{2,1},{3,2},{4,3},{5,4},{6,5},{7,6},{8,7},{9,8},{10,9},{11,1... | collective-permute-start | bytes 253448 | tf_op jit(solution)/shard_map/ppermute | solution.py:14
  57.1 14.3 %copy-start.10 = (f32[4,64,256]{2,1,0:T(8,128)}, f32[4,64,256]{2,1,0:T(8,128)S(1)}, u32[]{:S(2)}) copy-start(f32[4,64,256]{2,1,0:T(8,128)S(1)} %get-tuple-element.67) | copy-start | bytes 786436
  85.2 165.2 %all-to-all-start = ((f32[128,8,128]{2,1,0:T(8,128)}), f32[128,8,128]{2,1,0:T(8,128)}, u32[]{:S(2)}, u32[]{:S(2)}) async-start(f32[128,8,128]{2,1,0:T(8,128)} %bitcast_select_fusion), calls=%async_computation | async-start | bytes 1048576 | tf_op jit(solution)/shard_map/all_to_all | solution.py:169
  107.0 142.3 %copy-start.4 = (f32[2,4,64,256]{3,2,1,0:T(8,128)}, f32[2,4,64,256]{3,2,1,0:T(8,128)S(1)}, u32[]{:S(2)}) copy-start(f32[2,4,64,256]{3,2,1,0:T(8,128)S(1)} %pad_subtract_fusion.3) | copy-start | bytes 1572868
  249.5 3.0 copy-start.6
  249.5 3.0 copy-start.17
  249.8 2.8 copy-start.5
  250.4 3.1 %copy-start.21 = (s32[64,256]{1,0:T(8,128)S(1)}, s32[64,256]{1,0:T(8,128)}, u32[]{:S(2)}) copy-start(s32[64,256]{1,0:T(8,128)} %param.21) | copy-start | bytes 196612
  252.3 2.3 copy-start.25
  252.3 2.3 copy-start.26
  252.3 2.3 copy-start.27
  252.3 2.3 copy-start.28
  252.3 2.3 copy-start.32
  254.6 11.0 %copy-start.24 = (s32[256]{0:T(256)S(1)}, s32[256]{0:T(256)}, u32[]{:S(2)}) copy-start(s32[256]{0:T(256)} %copy-done.23) | copy-start | bytes 3076
  255.4 10.4 %copy-start.20 = (s32[128,2,2]{2,1,0:T(2,128)S(1)}, s32[128,2,2]{2,1,0:T(2,128)}, u32[]{:S(2)}) copy-start(s32[128,2,2]{2,1,0:T(2,128)} %iota_add_fusion.1) | copy-start | bytes 6148
  255.4 30.1 %copy-start.35 = (pred[1024]{0:T(1024)(128)(4,1)S(1)}, pred[1024]{0:T(1024)(128)(4,1)}, u32[]{:S(2)}) copy-start(pred[1024]{0:T(1024)(128)(4,1)} %fusion.121) | copy-start | bytes 3076
  257.0 28.5 %all-to-all-start.1 = ((f32[128,8,128]{2,1,0:T(8,128)}), f32[128,8,128]{2,1,0:T(8,128)S(1)}, u32[]{:S(2)}, u32[]{:S(2)}) async-start(f32[128,8,128]{2,1,0:T(8,128)} %fusion.17), calls=%async_computation.1 | async-start | bytes 1048576 | tf_op jit(solution)/shard_map/all_to_all | solution.py:213
  297.2 6.3 %collective-permute-start.5 = (f32[2,64,256]{2,1,0:T(8,128)S(1)}, f32[2,64,256]{2,1,0:T(8,128)S(1)}, u32[]{:S(2)}, u32[]{:S(2)}) collective-permute-start(f32[2,64,256]{2,1,0:T(8,128)S(1)} %reshape.713), channel_id=1, source_target_pairs={{128,0},{129,1},{130,2},{131,3},{132,4},{133,5},{134,6},{135,7},{1... | collective-permute-start | bytes 393224 | tf_op jit(solution)/shard_map/ppermute | solution.py:14
  (13 other events, 16.7 us)
Sparse Core Ops, SparseCore 0:
  11.6 225.6 all-gather.1
